TPU v7x, 512 devices: a whole 4x8x8 slice. The times are simulated.
512 devices in a mesh: row: 32 (over z, y_lo, core), col: 16 (over x, y_hi).
Axes of the slice: x: 4, y: 8 (y_hi: 4, y_lo: 2; y = y_hi * 2 + y_lo), z: 8, core: 2. Of those that a mesh axis runs over, the one named last changes fastest.
Arguments:
- inputs: float32 [2048, 8192], P('col', 'row'), may hold values from -6 to 6
- lang_ids: int32 [2048], P('row'), may hold values from 0 to 7
- group_table: int32 [8, 192], P(None, 'col'), may hold values 0 or 1
- cotangent: float32 [2048, 24576], P('row', 'col'), may hold values from -6 to 6
- weight: float32 [8192, 24576], P('row', 'col'), may hold values from -0.0390625 to 0.0390625
Outputs:
- weight_grad: float32 [8192, 24576], P('row', 'col')
- input_grad: float32 [2048, 8192], P('col', 'row')
All inputs are finite; a program needn't handle non-finite values. No bound on the sum of `group_table` on one device may be relied on, other than what follows from the above.
Results may differ from a plain program's by a relative error of at most 0.000092.
Values sent between devices are 32-bit elements; how exact they have to be, the bound alone decides.
A program may use at most 64 MiB of HBM per device.

v0:
```python
import jax
import jax.numpy as jnp
from jax import lax
from jax.sharding import PartitionSpec as P


def apply_groups(cotangent, lang_ids, group_table):
    labels = jnp.arange(group_table.shape[0], dtype=jnp.int32)
    onehot = (lang_ids[:, None] == labels[None, :]).astype(jnp.float32)
    group_rows = jnp.dot(
        onehot,
        group_table.astype(jnp.float32),
        preferred_element_type=jnp.float32,
        precision=lax.Precision.HIGHEST,
    )
    width = cotangent.shape[1] // group_table.shape[1]
    return cotangent * jnp.repeat(group_rows, width, axis=1)


def per_device(inputs, lang_ids, group_table, cotangent, weight):
    masked = apply_groups(cotangent, lang_ids, group_table)
    all_inputs = lax.all_gather(inputs, "col", axis=0, tiled=True)
    weight_grad = jnp.dot(
        all_inputs.T,
        lax.all_gather(masked, "row", axis=0, tiled=True),
        preferred_element_type=jnp.float32,
        precision=lax.Precision.HIGHEST,
    )
    partial_input = jnp.dot(
        lax.all_gather(masked, "row", axis=0, tiled=True),
        weight.T,
        preferred_element_type=jnp.float32,
        precision=lax.Precision.HIGHEST,
    )
    input_grad = lax.psum_scatter(partial_input, "col", scatter_dimension=0, tiled=True)
    return (weight_grad, input_grad)


def solution(mesh):
    placed = (P("col", "row"), P("row"), P(None, "col"), P("row", "col"), P("row", "col"))
    return jax.shard_map(
        per_device,
        mesh=mesh,
        in_specs=placed,
        out_specs=(P("row", "col"), P("col", "row")),
        check_vma=False,
    )
```

profile of v0, /device:TPU:1, one launch (start us, length us, event | category | flops | bytes accessed | tf_op | source)
XLA Modules:
  0.0 267.7 jit_solution(12663213769410164304)
XLA Ops:
  7.2 0.0 copy-start
  7.2 0.0 all-gather.3.cloned.1.call-start
  7.2 1.0 fusion
  8.2 0.2 broadcast_in_dim.2
  8.4 1.9 bitcast_multiply_fusion
  10.4 0.0 all-gather.3.cloned.1.call-update
  10.4 0.0 all-gather.5.cloned.1.call-start
  10.4 0.7 all-gather.5.cloned.1.call-update
  11.1 0.0 reduce-scatter.2.cloned.1.call-start
  11.2 88.7 %all-gather.3.cloned.1.call-done = f32[2048,1536]{1,0:T(8,128)} async-done(((f32[64,1536]{1,0:T(8,128)}), f32[2048,1536]{1,0:T(8,128)}) %all-gather.3.cloned.1.call-update) | async-done | bytes 12582928 | tf_op jit(solution)/shard_map/all_gather | solution.py:25
  99.9 0.0 copy-done
  99.9 13.5 %fusion.3 = f32[2048,256]{1,0:T(8,128)} fusion(f32[2048,1536]{1,0:T(8,128)} %all-gather.3.cloned.1.call-done, f32[256,1536]{1,0:T(8,128)S(1)} %copy-done), kind=kOutput, calls=%fused_computation.6 | convolution fusion | flops 9663676416 | bytes 16252928 | tf_op jit(solution)/shard_map/dot_general | solution.py:29
  113.4 0.0 reduce-scatter.2.cloned.1.call-update
  113.4 53.0 %all-gather.5.cloned.1.call-done = f32[2048,256]{1,0:T(8,128)} async-done(((f32[128,256]{1,0:T(8,128)}), f32[2048,256]{1,0:T(8,128)}) %all-gather.5.cloned.1.call-update) | async-done | bytes 2097168 | tf_op jit(solution)/shard_map/all_gather | solution.py:22
  166.4 23.0 %convolution_bitcast_fusion = f32[256,1536]{0,1:T(8,128)S(1)} fusion(f32[2048,1536]{1,0:T(8,128)} %all-gather.3.cloned.1.call-done, f32[2048,256]{1,0:T(8,128)} %all-gather.5.cloned.1.call-done), kind=kOutput, calls=%fused_computation | convolution fusion | flops 9663676416 | bytes 16252928 | tf_op jit(solution)/shard_map/dot_general | solution.py:23
  189.4 1.6 copy.10
  191.0 70.2 %reduce-scatter.2.cloned.1.call-done = f32[128,256]{1,0:T(8,128)} async-done(((f32[2048,256]{1,0:T(8,128)}), f32[128,256]{1,0:T(8,128)}) %reduce-scatter.2.cloned.1.call-update) | async-done | bytes 131088 | tf_op jit(solution)/shard_map/reduce_scatter | solution.py:35
Async XLA Ops:
  7.2 92.7 %copy-start = (f32[256,1536]{1,0:T(8,128)S(1)}, f32[256,1536]{1,0:T(8,128)}, u32[]{:S(2)}) copy-start(f32[256,1536]{1,0:T(8,128)} %param.9) | copy-start | bytes 4718596
  7.2 92.7 %all-gather.3.cloned.1.call-start = ((), (), s32[]{:S(2)}) async-start(), calls=%async_computation.1 | async-start | bytes 12976128 | tf_op jit(solution)/shard_map/all_gather | solution.py:25
  10.4 156.0 %all-gather.5.cloned.1.call-start = ((), (), s32[]{:S(2)}) async-start(), calls=%async_computation.2 | async-start | bytes 2228224 | tf_op jit(solution)/shard_map/all_gather | solution.py:22
  11.1 250.1 %reduce-scatter.2.cloned.1.call-start = ((), (), s32[]{:S(2)}) async-start(), calls=%async_computation.3 | async-start | bytes 2228224 | tf_op jit(solution)/shard_map/reduce_scatter | solution.py:35
Sparse Core Ops, SparseCore 0:
  10.7 89.0 all-gather.2
  102.9 63.4 all-gather.4
  171.1 90.0 reduce-scatter.1
where the time goes:
time: 268 us
  waiting for transfers between devices  213 us (79%)
  matrix products  37.5 us (14%)
  between operations  13.8 us (5%)
    all_gather x1, waiting for transfers between devices, per_device(): lax.all_gather(masked, 'row', axis=0, tiled=True)  88.7 us
    reduce_scatter x1, waiting for transfers between devices, per_device(): lax.psum_scatter(partial_input, 'col', scatter_dimension=0, tiled=True)  70.2 us
    all_gather x1, waiting for transfers between devices, per_device(): all_inputs = lax.all_gather(inputs, 'col', axis=0, tiled=True)  53 us
    dot_general x1, matrix products, per_device(): jnp.dot(all_inputs.T, lax.all_gather(masked, 'row', axis=0, tiled=True),...  23 us
    dot_general x1, matrix products, per_device(): jnp.dot(lax.all_gather(masked, 'row', axis=0, tiled=True), weight.T, pref...  13.5 us
  transfers between devices with their start and end apart: 3, of which 3 were waited for; matrix products, arithmetic and copies ran while one was open for 14% of the time, Pallas kernels for 0%

commit v1 on v0

v1 whole, which is shorter than its diff:
```python
import functools

import jax
import jax.numpy as jnp
from jax import lax
from jax.experimental import pallas as pl
from jax.experimental.pallas import tpu as pltpu
from jax.sharding import PartitionSpec as P

MESH = pl.DeviceIdType.MESH
BF16 = jnp.bfloat16
F32 = jnp.float32

STAGES = 4
ACROSS = 512
PIECE = 512
NZ, NX, NH = 8, 4, 4


def dot(a, b, dims):
    return lax.dot_general(a, b, (dims, ((), ())), preferred_element_type=F32)


def split(v):
    hi = v.astype(BF16)
    return hi, (v - hi.astype(F32)).astype(BF16)


def kernel(
    lang_hbm, table_hbm, g_hbm, x_hbm, w_hbm,
    dw_hbm, dx_hbm,
    lang, table, graw, w, gbuf, xbuf, pbuf, xrecv, ysum, yrecv, dxo,
    ghi, glo, whi, wlo, xthi, xtlo, dw,
    load_sem, zr, yr, kr, xh, xx, rx, ry, zs, ys, ks, xhs, xxs, rxs, rys, out_sem,
):
    S = gbuf.shape[0]
    T = gbuf.shape[4]
    F = gbuf.shape[5]
    M = 4 * NZ * T
    row, col = lax.axis_index("row"), lax.axis_index("col")
    z, l, k = row // 4, (row // 2) % 2, row % 2
    x, h = col // NH, col % NH
    ol, ok = 1 - l, 1 - k
    sg = 1 - 2 * k

    def at_row(dz, li, ki):
        return (((z + dz + NZ) % NZ) * 4 + li * 2 + ki, col)

    z1, z2 = at_row(sg, l, k), at_row(-sg, l, k)
    ypair, kpair = at_row(0, ol, k), at_row(0, l, ok)
    xdev = [(row, ((x + d) % NX) * NH + h) for d in (1, 3, 2)]
    hdev = [(row, x * NH + (h + d) % NH) for d in (1, 3, 2)]

    barrier = pltpu.get_barrier_semaphore()
    partners = [z1, z2, ypair, kpair] + xdev + hdev
    for p in partners:
        pl.semaphore_signal(barrier, inc=1, device_id=p, device_id_type=MESH)

    loads = [
        pltpu.make_async_copy(a, b, load_sem.at[i])
        for i, (a, b) in enumerate(
            ((lang_hbm, lang), (table_hbm, table), (g_hbm, graw), (w_hbm, w))
        )
    ]
    for c in loads:
        c.start()
    own_x = [pltpu.make_async_copy(x_hbm.at[i], xbuf.at[:, i, col], load_sem.at[4 + i]) for i in (0, 1)]
    for c in own_x:
        c.start()
    for c in loads[:3]:
        c.wait()
    labels = lax.broadcasted_iota(jnp.int32, (8, lang.shape[1]), 0)
    onehot = jnp.where(labels == lang[...], 1.0, 0.0).astype(F32)
    tab = table[...].astype(F32)
    wide = jnp.concatenate(
        [jnp.broadcast_to(tab[:, g : g + 1], (8, F // tab.shape[1])) for g in range(tab.shape[1])], axis=1
    )
    mask = dot(onehot, wide, ((0,), (0,)))
    masked = graw[...] * mask
    gbuf[:, k, z, l] = masked.reshape(S, T, F)
    for c in own_x:
        c.wait()
    pl.semaphore_wait(barrier, len(partners))

    def remote(src, dst, ssem, rsem, dev):
        return pltpu.make_async_remote_copy(
            src_ref=src, dst_ref=dst, send_sem=ssem, recv_sem=rsem, device_id=dev, device_id_type=MESH
        )

    def zsrc(dirn, d):
        return (z - sg * d + 2 * NZ) % NZ if dirn == 0 else (z + sg * d + 2 * NZ) % NZ

    reach = (NZ // 2, NZ // 2 - 1)

    def zcopy(s, dirn, d, which):
        zi = zsrc(dirn, d)
        ref = gbuf.at[s, k, zi, l] if which == 0 else gbuf.at[s, k, zi, ol, :, pl.ds(ACROSS, F - ACROSS)]
        return remote(ref, ref, zs.at[which], zr.at[s, dirn, d, which], z1 if dirn == 0 else z2)

    def zarrived(s, dirn, d, which):
        zi = zsrc(dirn, d)
        ref = gbuf.at[s, k, zi, l] if which == 0 else gbuf.at[s, k, zi, ol, :, pl.ds(ACROSS, F - ACROSS)]
        remote(ref, ref, zs.at[which], zr.at[s, dirn, d - 1, which], z1).wait_recv()

    def ycopy(s, dirn, d, to_me=False):
        li = ol if to_me else l
        zi = zsrc(dirn, d)
        ref = gbuf.at[s, k, zi, li] if d == 0 else gbuf.at[s, k, zi, li, :, pl.ds(0, ACROSS)]
        return remote(ref, ref, ys.at[0 if d == 0 else 1], yr.at[s, 0 if d == 0 else d + 4 * dirn], ypair)

    def kcopy(s, zi, ki):
        ref = gbuf.at[s, ki, zi]
        return remote(ref, ref, ks, kr.at[s, zi], kpair)

    def zsend(s, d, which):
        for dirn in (0, 1):
            if d < reach[dirn]:
                zcopy(s, dirn, d, which).start()

    def handle(s, d):
        for dirn in (0, 1):
            if d <= reach[dirn]:
                for which in (0, 1):
                    zarrived(s, dirn, d, which)
                    if d < reach[dirn]:
                        zcopy(s, dirn, d, which).start()
                ycopy(s, dirn, d).start()

    def kfin(s, d):
        for dirn in (0, 1):
            if d <= reach[dirn]:
                ycopy(s, dirn, d, True).wait_recv()
                kcopy(s, zsrc(dirn, d), k).start()

    def xh_copy(s, j):
        ref = xbuf.at[s, :, col]
        return remote(ref, ref, xhs, xh.at[s, j], hdev[j])

    def xx_copy(s, j):
        ref = xbuf.at[s, :, pl.ds(x * NH, NH)]
        return remote(ref, ref, xxs, xx.at[s, j], xdev[j])

    def rx_copy(s, j):
        xd = (x + (1, 3, 2)[j]) % NX
        return remote(pbuf.at[s, :, pl.ds(xd * NH, NH)], xrecv.at[s, j], rxs, rx.at[s, j], xdev[j])

    def ry_copy(s, j):
        hd = (h + (1, 3, 2)[j]) % NH
        return remote(ysum.at[s, :, hd], yrecv.at[s, j], rys, ry.at[s, j], hdev[j])

    def when(lo, i, hi):
        return pl.when(jnp.logical_and(i >= lo, i < hi))

    ycopy(0, 0, 0).start()
    zsend(0, 0, 0)
    for j in range(3):
        xh_copy(0, j).start()
    dw[...] = jnp.zeros_like(dw)
    loads[3].wait()
    for q in range(F // PIECE):
        sl = pl.ds(q * PIECE, PIECE)
        whi[:, sl], wlo[:, sl] = split(w[:, sl])

    def ppiece(s, q):
        sl = pl.ds(q * PIECE, PIECE)
        hi, lo = split(gbuf[s, :, :, :, :, sl].reshape(M, PIECE))
        ghi[:, sl] = hi
        glo[:, sl] = lo
        nt = ((1,), (1,))
        part = dot(hi, whi[:, sl], nt) + dot(lo, whi[:, sl], nt) + dot(hi, wlo[:, sl], nt)
        part = part.reshape(pbuf.shape[1:])
        if q == 0:
            pbuf[s] = part
        else:
            pbuf[s] += part

    def xprep(s):
        xt = xbuf[s].reshape(M, xbuf.shape[-1]).T
        xthi[...], xtlo[...] = split(xt)

    def wpiece(q):
        sl = pl.ds(q * PIECE, PIECE)
        nn = ((1,), (0,))
        dw[:, sl] += (
            dot(xthi[...], ghi[:, sl], nn) + dot(xtlo[...], ghi[:, sl], nn) + dot(xthi[...], glo[:, sl], nn)
        )

    def body(i, carry):
        @pl.when(i + 1 < S)
        def _():
            ycopy(i + 1, 0, 0).start()
            for j in range(3):
                xh_copy(i + 1, j).start()

        @when(2, i, S + 2)
        def _():
            kfin(i - 2, 3)
            handle(i - 2, 4)

        @pl.when(i < S)
        def _():
            ycopy(i, 0, 0, True).wait_recv()
            zsend(i, 0, 1)
            kcopy(i, z, k).start()

        @when(1, i, S + 1)
        def _():
            handle(i - 1, 2)

        @pl.when(i + 1 < S)
        def _():
            zsend(i + 1, 0, 0)

        @pl.when(i < S)
        def _():
            for j in range(3):
                xh_copy(i, j).wait_recv()
            for j in range(3):
                xx_copy(i, j).start()

        @when(2, i, S + 2)
        def _():
            s = i - 2
            kfin(s, 4)
            for zi in range(NZ):
                kcopy(s, zi, ok).wait_recv()
            for q in range(F // PIECE):
                ppiece(s, q)

        @pl.when(i < S)
        def _():
            handle(i, 1)

        @when(1, i, S + 1)
        def _():
            kfin(i - 1, 2)

        @when(2, i, S + 2)
        def _():
            s = i - 2
            for j in range(3):
                rx_copy(s, j).start()
            for j in range(3):
                xx_copy(s, j).wait_recv()
            xprep(s)
            for q in range(F // PIECE):
                wpiece(q)

        @pl.when(i == S + 1)
        def _():
            pltpu.make_async_copy(dw, dw_hbm, out_sem.at[0]).start()

        @when(1, i, S + 1)
        def _():
            handle(i - 1, 3)

        @pl.when(i < S)
        def _():
            kfin(i, 1)

        @when(4, i, S + 4)
        def _():
            s = i - 4
            for j in range(3):
                ry_copy(s, j).wait_recv()
            dxo[:, s] = (ysum[s, :, h] + yrecv[s, 0]) + (yrecv[s, 1] + yrecv[s, 2])

        @when(3, i, S + 3)
        def _():
            s = i - 3
            for j in range(3):
                rx_copy(s, j).wait_recv()
            ysum[s] = (pbuf[s, :, pl.ds(x * NH, NH)] + xrecv[s, 0]) + (xrecv[s, 1] + xrecv[s, 2])
            for j in range(3):
                ry_copy(s, j).start()

        return carry

    lax.fori_loop(0, S + 4, body, 0)
    pltpu.make_async_copy(dxo, dx_hbm, out_sem.at[1]).start()

    def drain(ref, sem):
        remote(ref, ref, sem, sem, z1).wait_send()

    far = NZ - 1
    drain(gbuf.at[:, 0, pl.ds(0, far), 0], zs.at[0])
    drain(gbuf.at[:, 0, pl.ds(0, far), 0, :, pl.ds(ACROSS, F - ACROSS)], zs.at[1])
    drain(gbuf.at[:, 0, 0, 0], ys.at[0])
    drain(gbuf.at[:, 0, pl.ds(0, far), 0, :, pl.ds(0, ACROSS)], ys.at[1])
    drain(gbuf.at[:, 0], ks)
    drain(xbuf.at[:, :, pl.ds(0, 3)], xhs)
    drain(xbuf.at[:, :, pl.ds(0, 3 * NH)], xxs)
    drain(xrecv, rxs)
    drain(yrecv, rys)
    pltpu.make_async_copy(dw, dw_hbm, out_sem.at[0]).wait()
    pltpu.make_async_copy(dxo, dx_hbm, out_sem.at[1]).wait()


def per_device(inputs, lang_ids, group_table, cotangent, weight):
    S = STAGES
    tokens, F = cotangent.shape
    D = inputs.shape[1]
    T = tokens // S
    M = 4 * NZ * T
    xin = inputs.reshape(2, S, T, D)
    anywhere = pl.BlockSpec(memory_space=pl.ANY)
    dma = pltpu.SemaphoreType.DMA
    dw, dx = pl.pallas_call(
        kernel,
        name="backward",
        out_shape=(
            jax.ShapeDtypeStruct((D, F), F32),
            jax.ShapeDtypeStruct((2, S, T, D), F32),
        ),
        in_specs=[anywhere] * 5,
        out_specs=(anywhere, anywhere),
        scratch_shapes=[
            pltpu.VMEM((1, tokens), jnp.int32),
            pltpu.VMEM(group_table.shape, jnp.int32),
            pltpu.VMEM((tokens, F), F32),
            pltpu.VMEM((D, F), F32),
            pltpu.VMEM((S, 2, NZ, 2, T, F), F32),
            pltpu.VMEM((S, 2, NX * NH, T, D), F32),
            pltpu.VMEM((S, 2, NX * NH, T, D), F32),
            pltpu.VMEM((S, 3, 2, NH, T, D), F32),
            pltpu.VMEM((S, 2, NH, T, D), F32),
            pltpu.VMEM((S, 3, 2, T, D), F32),
            pltpu.VMEM((2, S, T, D), F32),
            pltpu.VMEM((M, F), BF16),
            pltpu.VMEM((M, F), BF16),
            pltpu.VMEM((D, F), BF16),
            pltpu.VMEM((D, F), BF16),
            pltpu.VMEM((D, M), BF16),
            pltpu.VMEM((D, M), BF16),
            pltpu.VMEM((D, F), F32),
            dma((6,)),
            dma((S, 2, NZ // 2, 2)),
            dma((S, NZ)),
            dma((S, NZ)),
            dma((S, 3)),
            dma((S, 3)),
            dma((S, 3)),
            dma((S, 3)),
            dma((2,)),
            dma((2,)),
            dma,
            dma,
            dma,
            dma,
            dma,
            dma((2,)),
        ],
        compiler_params=pltpu.CompilerParams(
            collective_id=0, has_side_effects=True, vmem_limit_bytes=60 * 2**20
        ),
    )(lang_ids.reshape(1, tokens), group_table, cotangent, xin, weight)
    return dw, dx.reshape(2 * tokens, D)


def solution(mesh):
    placed = (P("col", "row"), P("row"), P(None, "col"), P("row", "col"), P("row", "col"))
    return jax.shard_map(
        per_device,
        mesh=mesh,
        in_specs=placed,
        out_specs=(P("row", "col"), P("col", "row")),
        check_vma=False,
    )
```

time: 268 us -> 106 us (0.40)
  waiting for transfers between devices: 213 us -> 0 us
  Pallas kernels: 0 us -> 102 us
  matrix products: 37.5 us -> 0 us
  between operations: 13.8 us -> 0.65 us
    all_gather x2 -> x0, waiting for transfers between devices: 142 us -> none  [the longest x1 88.7 us: per_device(): lax.all_gather(masked, 'row', axis=0, tiled=True)]
    pallas_call x0 -> x1, Pallas kernels: none -> 102 us  [per_device(): pl.pallas_call(kernel, name='backward', out_shape=(jax.ShapeDtypeStruct((...]
    reduce_scatter x1 -> x0, waiting for transfers between devices: 70.2 us -> none  [per_device(): lax.psum_scatter(partial_input, 'col', scatter_dimension=0, tiled=True)]
    dot_general x3 -> x0, matrix products: 37.5 us -> none  [the longest x1 23 us: per_device(): jnp.dot(all_inputs.T, lax.all_gather(masked, 'row', axis=0, tiled=True),...]
  transfers between devices with their start and end apart: 3 -> 0, of which waited for: 3 -> 0; matrix products, arithmetic and copies ran while one was open for 14% -> 0% of each run, Pallas kernels for 0% -> 0%
where the time goes in v1:
time: 106 us
  Pallas kernels  102 us (96%)
  local copies, waits for them, and re-layouts  3.35 us (3%)
    pallas_call x1, Pallas kernels, per_device(): pl.pallas_call(kernel, name='backward', out_shape=(jax.ShapeDtypeStruct((...  102 us
    unnamed x4, local copies, waits for them, and re-layouts  3.35 us

profile of v1, /device:TPU:1, one launch (start us, length us, event | category | flops | bytes accessed | tf_op | source)
XLA Modules:
  0.0 106.0 jit_solution(9117330094019661194)
XLA Ops:
  0.6 102.0 %backward.1 = (f32[256,1536]{1,0:T(8,128)}, f32[2,4,16,256]{3,2,1,0:T(8,128)}) custom-call(s32[1,64]{1,0:T(1,128)} %bitcast.5, s32[8,12]{1,0:T(8,128)} %table_hbm.1, f32[64,1536]{1,0:T(8,128)} %g_hbm.1, f32[2,4,16,256]{3,2,1,0:T(8,128)} %bitcast.3, f32[256,1536]{1,0:T(8,128)} %w_hbm.1), custom_call_target="tpu_custom_call" | custom-call | tf_op jit(solution)/shard_map/backward/pallas_call | solution.py:308
  102.6 0.0 copy-start
  102.6 2.7 %copy.9 = f32[256,1536]{1,0:T(8,128)} copy(f32[256,1536]{1,0:T(8,128)} %get-tuple-element.8) | data formatting | bytes 3145728
  105.3 0.0 copy-done
  105.3 0.7 copy.10
Async XLA Ops:
  102.6 2.7 %copy-start = (f32[2,4,16,256]{3,2,1,0:T(8,128)S(1)}, f32[2,4,16,256]{3,2,1,0:T(8,128)}, u32[]{:S(2)}) copy-start(f32[2,4,16,256]{3,2,1,0:T(8,128)} %get-tuple-element.5) | copy-start | bytes 393220
